TPU v7x, 32 devices: a whole 2x2x4 slice. The times are simulated.
32 devices in a mesh: cluster: 8 (over y, x, core), matrix: 4 (over z).
Axes of the slice: x: 2, y: 2, z: 4, core: 2. Of those that a mesh axis runs over, the one named last changes fastest.
Arguments:
- matrix_pressure_iterate: float32 [32768, 128], P(('cluster', 'matrix')), may hold values from 0 to 2
- matrix_water_saturation: float32 [32768, 128], P(('cluster', 'matrix')), may hold values from 0.05 to 0.95
- matrix_pressure_prior: float32 [32768, 128], P(('cluster', 'matrix')), may hold values from 0 to 2
- matrix_saturation_prior: float32 [32768, 128], P(('cluster', 'matrix')), may hold values from 0.05 to 0.95
- matrix_pore_volume: float32 [32768, 128], P(('cluster', 'matrix')), may hold values from 0.5 to 5
- cell_shape_factor: float32 [32768, 128], P(('cluster', 'matrix')), may hold values from 0.2 to 5
- fracture_pressure: float32 [1024, 128], P(('cluster', 'matrix')), may hold values from 0 to 2
- fracture_saturation: float32 [1024, 128], P(('cluster', 'matrix')), may hold values from 0.05 to 0.95
- fracture_pressure_old: float32 [1024, 128], P(('cluster', 'matrix')), may hold values from 0 to 2
- fracture_saturation_old: float32 [1024, 128], P(('cluster', 'matrix')), may hold values from 0.05 to 0.95
- fracture_pore: float32 [1024, 128], P(('cluster', 'matrix')), may hold values from 0.05 to 0.5
- fracture_trans: float32 [1024, 128], P(('cluster', 'matrix')), may hold values from 0.5 to 10
- feeding_owner_group: int32 [32768, 1], P(('cluster', 'matrix')), may hold values from 0 to 7; in each aligned block of 1024 rows (0 to 1023, 1024 to 2047, ...) at most 256 rows name the same one
- owner_tile_position: int32 [32768], P(('cluster', 'matrix')), may hold values from 0 to 127
Outputs:
- matrix_residual: float32 [2, 32768, 128], P(None, ('cluster', 'matrix'))
- fracture_residual: float32 [2, 1024, 128], P(None, ('cluster', 'matrix'))
- jacobian: float32 [4, 32768, 128], P(None, ('cluster', 'matrix'))
Inputs may be any that keep to these rules, and one draw needn't show every extreme that they name: `feeding_owner_group`: among the rows of one device, each owner group is named by at most 256 rows, a bound that some block reaches.
All inputs are finite; a program needn't handle non-finite values. Where the computation divides by a largest or mean magnitude, that divisor is 1e-20 or more.
Results may differ from a plain program's by a relative error of at most 0.0003.
Values sent between devices are 32-bit elements; how exact they have to be, the bound alone decides.
No kernel may reach another device: no remote copies, remote signals or barrier semaphores. Data moves between devices by JAX's collectives and lax.ppermute only.
A program may use at most 64 MiB of HBM per device.

v0:
```python
import jax
import jax.numpy as jnp
from jax import lax
from jax.sharding import PartitionSpec as P

VISC_WATER = 1.0
VISC_OIL = 3.0
ROCK_COMPRESS = 0.1
EPSILON = 1e-06
HIGHEST = lax.Precision.HIGHEST


def mobility(saturation):
    return (
        saturation * saturation / VISC_WATER,
        (1.0 - saturation) * (1.0 - saturation) / VISC_OIL,
    )


def storage(pressure, saturation, pressure_old, saturation_old, pore):
    factor = 1.0 + ROCK_COMPRESS * pressure
    factor_old = 1.0 + ROCK_COMPRESS * pressure_old
    water = pore * (factor * saturation - factor_old * saturation_old)
    oil = pore * (factor * (1.0 - saturation) - factor_old * (1.0 - saturation_old))
    return (water, oil, factor)


def chain_flow(pressure, saturation, trans):
    drop = pressure[:, :-1] - pressure[:, 1:]
    upwind = jnp.where(drop >= 0.0, saturation[:, :-1], saturation[:, 1:])
    water_mob, oil_mob = mobility(upwind)
    links = trans[:, :-1]
    water = links * water_mob * drop
    oil = links * oil_mob * drop

    def net_flow(flow):
        return jnp.pad(flow, ((0, 0), (0, 1))) - jnp.pad(flow, ((0, 0), (1, 0)))

    return (net_flow(water), net_flow(oil))


def per_device(
    matrix_pressure_iterate,
    matrix_water_saturation,
    matrix_pressure_prior,
    matrix_saturation_prior,
    matrix_pore_volume,
    cell_shape_factor,
    fracture_pressure,
    fracture_saturation,
    fracture_pressure_old,
    fracture_saturation_old,
    fracture_pore,
    fracture_trans,
    feeding_owner_group,
    owner_tile_position,
):
    groups = lax.axis_size("cluster")
    members = lax.axis_size("matrix")
    local_tiles = matrix_pressure_iterate.shape[0]
    frac_tiles = fracture_pressure.shape[0]
    width = matrix_pressure_iterate.shape[1]
    capacity = max(2, 2 * local_tiles // groups)
    slot_count = groups * capacity
    group_tiles = frac_tiles * members
    target_group = feeding_owner_group[:, 0]
    member_table = (target_group[:, None] == jnp.arange(groups, dtype=jnp.int32)[None, :]).astype(
        jnp.int32
    )
    ranks = jnp.sum((jnp.cumsum(member_table, axis=0) - member_table) * member_table, axis=1)
    position = target_group * capacity + ranks
    placing = position[None, :] == jnp.arange(slot_count, dtype=jnp.int32)[:, None]
    selector = placing.astype(jnp.float32)
    requested = jnp.sum(jnp.where(placing, owner_tile_position[None, :] + 1, 0), axis=1) - 1
    incoming = lax.all_to_all(
        requested.reshape(groups, capacity), "cluster", split_axis=0, concat_axis=0, tiled=True
    ).reshape(slot_count)
    lookup = (incoming[:, None] == jnp.arange(group_tiles, dtype=jnp.int32)[None, :]).astype(
        jnp.float32
    )
    store_water, store_oil, factor = storage(
        matrix_pressure_iterate,
        matrix_water_saturation,
        matrix_pressure_prior,
        matrix_saturation_prior,
        matrix_pore_volume,
    )
    base_wp = matrix_pore_volume * ROCK_COMPRESS * matrix_water_saturation
    base_ws = matrix_pore_volume * factor
    base_op = matrix_pore_volume * ROCK_COMPRESS * (1.0 - matrix_water_saturation)
    base_os = -matrix_pore_volume * factor
    own_state = jnp.concatenate([fracture_pressure, fracture_saturation], axis=1)
    everything = lax.all_gather(own_state, ("cluster", "matrix"), axis=0, tiled=True)
    global_owner = target_group * group_tiles + owner_tile_position
    owner_state = jnp.take(everything, global_owner, axis=0)
    other_pressure = owner_state[:, :width]
    other_saturation = owner_state[:, width:]
    drop = matrix_pressure_iterate - other_pressure
    upstream = drop >= 0.0
    upwind = jnp.where(upstream, matrix_water_saturation, other_saturation)
    water_mob, oil_mob = mobility(upwind)
    water_flow = cell_shape_factor * water_mob * drop
    oil_flow = cell_shape_factor * oil_mob * drop
    matrix_water = store_water + water_flow
    matrix_oil = store_oil + oil_flow
    jac_wp = base_wp + cell_shape_factor * water_mob
    jac_ws = base_ws + jnp.where(
        upstream, cell_shape_factor * 2.0 * matrix_water_saturation / VISC_WATER * drop, 0.0
    )
    jac_op = base_op + cell_shape_factor * oil_mob
    jac_os = base_os + jnp.where(
        upstream, -cell_shape_factor * 2.0 * (1.0 - matrix_water_saturation) / VISC_OIL * drop, 0.0
    )
    matrix_top = jnp.stack([jnp.max(jnp.abs(matrix_water)), jnp.max(jnp.abs(matrix_oil))])
    packed = jnp.concatenate([water_flow, oil_flow], axis=1)
    slot_terms = jnp.dot(selector, packed, precision=HIGHEST)
    arrived = lax.all_to_all(
        slot_terms.reshape(groups, capacity, 2 * width),
        "cluster",
        split_axis=0,
        concat_axis=0,
        tiled=True,
    ).reshape(slot_count, 2 * width)
    flow_sums = lax.psum_scatter(
        jnp.einsum("sf,sc->fc", lookup, arrived, precision=HIGHEST),
        "matrix",
        scatter_dimension=0,
        tiled=True,
    )
    frac_water, frac_oil, frac_factor = storage(
        fracture_pressure,
        fracture_saturation,
        fracture_pressure_old,
        fracture_saturation_old,
        fracture_pore,
    )
    net_water, net_oil = chain_flow(fracture_pressure, fracture_saturation, fracture_trans)
    fracture_water = frac_water + net_water - flow_sums[:, :width]
    fracture_oil = frac_oil + net_oil - flow_sums[:, width:]
    fracture_top = jnp.stack([jnp.max(jnp.abs(fracture_water)), jnp.max(jnp.abs(fracture_oil))])
    overall = lax.pmax(jnp.maximum(matrix_top, fracture_top), ("cluster", "matrix"))
    scale_water = overall[0] + EPSILON
    scale_oil = overall[1] + EPSILON
    matrix_residual = jnp.stack([matrix_water / scale_water, matrix_oil / scale_oil])
    fracture_residual = jnp.stack([fracture_water / scale_water, fracture_oil / scale_oil])
    jacobian = jnp.stack([jac_wp, jac_ws, jac_op, jac_os])
    return (matrix_residual, fracture_residual, jacobian)


def solution(mesh):
    placed = (
        P(("cluster", "matrix"), None),
        P(("cluster", "matrix"), None),
        P(("cluster", "matrix"), None),
        P(("cluster", "matrix"), None),
        P(("cluster", "matrix"), None),
        P(("cluster", "matrix"), None),
        P(("cluster", "matrix"), None),
        P(("cluster", "matrix"), None),
        P(("cluster", "matrix"), None),
        P(("cluster", "matrix"), None),
        P(("cluster", "matrix"), None),
        P(("cluster", "matrix"), None),
        P(("cluster", "matrix"), None),
        P(("cluster", "matrix")),
    )
    return jax.shard_map(
        per_device,
        mesh=mesh,
        in_specs=placed,
        out_specs=(
            P(None, ("cluster", "matrix"), None),
            P(None, ("cluster", "matrix"), None),
            P(None, ("cluster", "matrix"), None),
        ),
        check_vma=False,
    )
```

profile of v0, /device:TPU:0, one launch (start us, length us, event | category | flops | bytes accessed | tf_op | source)
XLA Modules:
  0.0 185.6 jit_solution(14330601744383255682)
XLA Ops:
  7.2 0.0 all-gather.2.cloned.1.call-start
  7.2 1.4 pad_maximum_fusion.2
  8.6 0.0 all-gather.2.cloned.1.call-update
  8.6 0.7 fusion.12
  9.3 2.3 %reduce-window.6 = s32[8,8,128]{2,1,0:T(8,128)S(1)} reduce-window(s32[8,8,128]{2,1,0:T(8,128)S(1)} %fusion.12, s32[]{:T(128)} %constant.20.clone.1), window={size=1x1x128 pad=0_0x0_0x127_0}, to_apply=%region_2.3 | reduce-window | flops 1040384 | bytes 65540 | tf_op jit(solution)/shard_map/reduce-window
  11.5 0.3 slice_reduce_fusion
  11.8 0.2 reduce-window.9
  12.0 0.1 add_bitcast_fusion.4
  12.1 0.7 fusion.11
  12.8 0.7 broadcast_add_fusion.1
  13.5 0.9 select_reduce_fusion
  14.4 0.6 broadcast_add_fusion
  15.0 5.2 %all-to-all-start = ((s32[8,1,256]{2,1,0:T(1,128)}), s32[8,1,256]{2,1,0:T(1,128)S(1)}, u32[]{:S(2)}, u32[]{:S(2)}) async-start(s32[8,1,256]{2,1,0:T(1,128)} %bitcast.5), calls=%async_computation | async-start | bytes 16384 | tf_op jit(solution)/shard_map/all_to_all | solution.py:75
  20.2 0.0 reduce-scatter.2.cloned.1.call-start
  20.3 0.7 compare_and_fusion
  21.0 47.1 %all-gather.2.cloned.1.call-done = f32[1024,256]{1,0:T(8,128)} async-done(((f32[32,256]{1,0:T(8,128)}), f32[1024,256]{1,0:T(8,128)}) %all-gather.2.cloned.1.call-update) | async-done | bytes 1048592 | tf_op jit(solution)/shard_map/all_gather | solution.py:93
  68.1 4.7 %gather_fusion = f32[1024,256]{1,0:T(8,128)S(1)} fusion(f32[1024,256]{1,0:T(8,128)} %all-gather.2.cloned.1.call-done, s32[1024]{0:T(1024)S(1)} %get-tuple-element.26), kind=kCustom, calls=%fused_computation | custom fusion | bytes 2101248 | tf_op jit(solution)/shard_map/jit(_take)/gather | solution.py:95
  72.8 0.0 copy-start
  72.8 0.0 copy-start.1
  72.8 0.0 copy-start.2
  72.8 0.0 copy-start.3
  72.8 0.2 broadcast_select_fusion
  73.0 0.8 copy-done
  73.8 0.2 copy-done.1
  74.0 0.2 copy-done.2
  74.2 0.2 copy-done.3
  74.3 0.0 copy-start.8
  74.3 0.0 copy-start.9
  74.3 1.0 add_bitcast_fusion.3
  75.3 0.0 copy-done.8
  75.4 0.3 copy-done.9
  75.7 2.5 %abs_reduce_fusion.1 = (f32[]{:T(128)}, f32[1024,128]{1,0:T(8,128)S(1)}, f32[1024,128]{1,0:T(8,128)S(1)}, f32[]{:T(128)}, f32[1024,128]{1,0:T(8,128)S(1)}, /*ind...) fusion(f32[1024,128]{1,0:T(8,128)S(1)} %copy-done, ...), kind=kLoop, calls=%fused_computation.24 | loop fusion | flops 6291454 | bytes 7864328 | tf_op jit(solution)/shard_map/reduce_max | solution.py:114
  78.2 4.0 %fusion = f32[2048,256]{1,0:T(8,128)S(1)} fusion(s32[1024]{0:T(1024)S(1)} %get-tuple-element.27, f32[1024,128]{1,0:T(8,128)S(1)} %get-tuple-element.17, f32[1024,128]{1,0:T(8,128)S(1)} %get-tuple-element.11), kind=kOutput, calls=%fused_computation.3 | convolution fusion | flops 6444810240 | bytes 3149824 | tf_op jit(solution)/shard_map/dot_general | solution.py:116
  82.2 0.0 all-to-all-done
  82.2 29.2 %all_to_all.11 = f32[8,256,256]{2,1,0:T(8,128)S(1)} all-to-all(f32[8,256,256]{2,1,0:T(8,128)S(1)} %bitcast.49), channel_id=1, replica_groups=mesh['cluster'=8,'matrix'=4] {'cluster'}, dimensions={0} | all-to-all | bytes 4194304 | tf_op jit(solution)/shard_map/all_to_all | solution.py:117
  111.4 0.0 copy-start.10
  111.4 0.0 copy-start.14
  111.4 0.0 copy-start.15
  111.4 0.0 copy-start.4
  111.5 0.0 copy-start.5
  111.5 0.0 copy-start.6
  111.5 0.0 copy-start.7
  111.5 2.2 %fusion.5 = f32[128,256]{1,0:T(8,128)} fusion(f32[2048,256]{1,0:T(8,128)S(1)} %bitcast.48, s32[2048]{0:T(1024)S(1)} %bitcast.54), kind=kOutput, calls=%fused_computation.11 | convolution fusion | flops 805568512 | bytes 2236416 | tf_op jit(solution)/shard_map/sf,sc->fc/dot_general | solution.py:125
  113.7 0.0 reduce-scatter.2.cloned.1.call-update
  113.7 0.0 copy-done.10
  113.7 0.0 copy-done.11
  113.7 0.0 copy-done.12
  113.7 0.1 multiply_multiply_fusion.3
  113.8 17.5 %reduce-scatter.2.cloned.1.call-done = f32[32,256]{1,0:T(8,128)} async-done(((f32[128,256]{1,0:T(8,128)}), f32[32,256]{1,0:T(8,128)}) %reduce-scatter.2.cloned.1.call-update) | async-done | bytes 32784 | tf_op jit(solution)/shard_map/reduce_scatter | solution.py:124
  131.3 0.0 copy-done.13
  131.3 0.0 copy-done.14
  131.3 0.0 copy-done.15
  131.3 1.5 abs_reduce_fusion.3
  132.8 2.6 %maximum_maximum_fusion = f32[2]{0:T(128)S(1)} fusion(f32[1]{0:T(128)} %bitcast.2, f32[1]{0:T(128)} %bitcast.1, f32[1]{0:T(128)} %bitcast.10, f32[1]{0:T(128)} %bitcast.9), kind=kLoop, calls=%fused_computation.62 | loop fusion | flops 6 | bytes 24 | tf_op jit(solution)/shard_map/max | solution.py:141
  135.3 0.0 copy-done.4
  135.3 0.0 copy-done.5
  135.4 0.0 copy-done.6
  135.4 0.0 copy-done.7
  135.4 1.5 pad_maximum_fusion
  136.8 38.3 %pmax.7 = f32[2]{0:T(128)S(1)} all-reduce(f32[2]{0:T(128)S(1)} %maximum_maximum_fusion), channel_id=1, replica_groups=mesh['cluster'=8,'matrix'=4] {'cluster','matrix'}, use_global_device_ids=true, to_apply=%region_9.10 | all-reduce | flops 2 | bytes 16 | tf_op jit(solution)/shard_map/pmax | solution.py:141
  175.2 0.6 fusion.16
  177.1 0.6 pad_maximum_fusion.3
  177.7 0.1 divide_bitcast_fusion
  177.8 1.0 pad_maximum_fusion.1
  (4 shorter events, 0.0 us)
Async XLA Ops:
  7.2 60.9 %all-gather.2.cloned.1.call-start = ((), (), s32[]{:S(2)}) async-start(), calls=%async_computation.3 | async-start | bytes 1081344 | tf_op jit(solution)/shard_map/all_gather | solution.py:93
  15.0 67.2 %all-to-all-start = ((s32[8,1,256]{2,1,0:T(1,128)}), s32[8,1,256]{2,1,0:T(1,128)S(1)}, u32[]{:S(2)}, u32[]{:S(2)}) async-start(s32[8,1,256]{2,1,0:T(1,128)} %bitcast.5), calls=%async_computation | async-start | bytes 16384 | tf_op jit(solution)/shard_map/all_to_all | solution.py:75
  20.2 111.1 %reduce-scatter.2.cloned.1.call-start = ((), (), s32[]{:S(2)}) async-start(), calls=%async_computation.4 | async-start | bytes 163840 | tf_op jit(solution)/shard_map/reduce_scatter | solution.py:124
  72.8 1.0 copy-start
  72.8 1.2 copy-start.1
  72.8 1.3 copy-start.2
  72.8 1.5 copy-start.3
  74.3 1.0 copy-start.8
  74.3 1.4 copy-start.9
  111.4 2.3 %copy-start.10 = (f32[32,128]{1,0:T(8,128)S(1)}, f32[32,128]{1,0:T(8,128)}, u32[]{:S(2)}) copy-start(f32[32,128]{1,0:T(8,128)} %param.21) | copy-start | bytes 49156
  111.4 2.3 %copy-start.11 = (f32[32,128]{1,0:T(8,128)S(1)}, f32[32,128]{1,0:T(8,128)}, u32[]{:S(2)}) copy-start(f32[32,128]{1,0:T(8,128)} %param.20) | copy-start | bytes 49156
  111.4 2.3 %copy-start.12 = (f32[32,128]{1,0:T(8,128)S(1)}, f32[32,128]{1,0:T(8,128)}, u32[]{:S(2)}) copy-start(f32[32,128]{1,0:T(8,128)} %param.25) | copy-start | bytes 49156
  111.4 19.9 %copy-start.13 = (f32[32,128]{1,0:T(8,128)S(1)}, f32[32,128]{1,0:T(8,128)}, u32[]{:S(2)}) copy-start(f32[32,128]{1,0:T(8,128)} %param.24) | copy-start | bytes 49156
  111.4 19.8 %copy-start.14 = (f32[32,128]{1,0:T(8,128)S(1)}, f32[32,128]{1,0:T(8,128)}, u32[]{:S(2)}) copy-start(f32[32,128]{1,0:T(8,128)} %param.23) | copy-start | bytes 49156
  111.4 19.8 %copy-start.15 = (f32[32,128]{1,0:T(8,128)S(1)}, f32[32,128]{1,0:T(8,128)}, u32[]{:S(2)}) copy-start(f32[32,128]{1,0:T(8,128)} %param.22) | copy-start | bytes 49156
  111.4 23.9 %copy-start.4 = (f32[1,1024,128]{2,1,0:T(8,128)S(1)}, f32[1,1024,128]{2,1,0:T(8,128)}, u32[]{:S(2)}) copy-start(f32[1,1024,128]{2,1,0:T(8,128)} %get-tuple-element.18) | copy-start | bytes 1572868
  111.5 23.9 %copy-start.5 = (f32[1,1024,128]{2,1,0:T(8,128)S(1)}, f32[1,1024,128]{2,1,0:T(8,128)}, u32[]{:S(2)}) copy-start(f32[1,1024,128]{2,1,0:T(8,128)} %get-tuple-element.19) | copy-start | bytes 1572868
  111.5 23.9 %copy-start.6 = (f32[1,1024,128]{2,1,0:T(8,128)S(1)}, f32[1,1024,128]{2,1,0:T(8,128)}, u32[]{:S(2)}) copy-start(f32[1,1024,128]{2,1,0:T(8,128)} %get-tuple-element.20) | copy-start | bytes 1572868
  111.5 23.9 %copy-start.7 = (f32[1,1024,128]{2,1,0:T(8,128)S(1)}, f32[1,1024,128]{2,1,0:T(8,128)}, u32[]{:S(2)}) copy-start(f32[1,1024,128]{2,1,0:T(8,128)} %get-tuple-element.3) | copy-start | bytes 1572868
Sparse Core Ops, SparseCore 0:
  11.5 56.5 all-gather.1
  113.8 17.4 reduce-scatter.1
where the time goes:
time: 187 us; the launch traced here: 186 us
  blocking collectives  67.5 us (36%)
  waiting for transfers between devices  64.6 us (35%)
  other arithmetic  19.3 us (10%)
  between operations  15.5 us (8%)
  local copies, waits for them, and re-layouts  7.26 us (4%)
  matrix products  6.16 us (3%)
  starting transfers between devices  5.27 us (3%)
    all_gather x1, waiting for transfers between devices, per_device(): lax.all_gather(own_state, ('cluster', 'matrix'), axis=0, tiled=True)  47.1 us
    pmax x1, blocking collectives, per_device(): lax.pmax(jnp.maximum(matrix_top, fracture_top), ('cluster', 'matrix'))  38.3 us
    all_to_all x1, blocking collectives, per_device(): lax.all_to_all(slot_terms.reshape(groups, capacity, 2 * width), 'cluster'...  29.2 us
    reduce_scatter x1, waiting for transfers between devices, per_device(): lax.psum_scatter(jnp.einsum('sf,sc->fc', lookup, arrived, precision=HIGHE...  17.5 us
    all_to_all x1, starting transfers between devices, per_device(): lax.all_to_all(requested.reshape(groups, capacity), 'cluster', split_axis...  5.2 us
    gather x1, local copies, waits for them, and re-layouts, per_device(): owner_state = jnp.take(everything, global_owner, axis=0)  4.68 us
    dot_general x1, matrix products, per_device(): slot_terms = jnp.dot(selector, packed, precision=HIGHEST)  4 us
  transfers between devices with their start and end apart: 3, of which 2 were waited for; matrix products, arithmetic and copies ran while one was open for 11% of the time, Pallas kernels for 0%

commit v1 on v0

v1 whole, which is shorter than its diff:
```python
import functools

import jax
import jax.numpy as jnp
from jax import lax
from jax.experimental import pallas as pl
from jax.experimental.pallas import tpu as pltpu
from jax.sharding import PartitionSpec as P

VISC_WATER = 1.0
VISC_OIL = 3.0
ROCK_COMPRESS = 0.1
EPSILON = 1e-06
LIFT = 2.0**64
VMEM = pl.BlockSpec(memory_space=pltpu.VMEM)
SMEM = pl.BlockSpec(memory_space=pltpu.SMEM)
F32 = jnp.float32
BF16 = jnp.bfloat16


def params(mib):
    return pltpu.CompilerParams(vmem_limit_bytes=mib << 20)


def struct(*shape, dtype=F32):
    return jax.ShapeDtypeStruct(shape, dtype)


def mobility(saturation):
    return (
        saturation * saturation / VISC_WATER,
        (1.0 - saturation) * (1.0 - saturation) / VISC_OIL,
    )


def storage(pressure, saturation, pressure_old, saturation_old, pore):
    factor = 1.0 + ROCK_COMPRESS * pressure
    factor_old = 1.0 + ROCK_COMPRESS * pressure_old
    water = pore * (factor * saturation - factor_old * saturation_old)
    oil = pore * (factor * (1.0 - saturation) - factor_old * (1.0 - saturation_old))
    return (water, oil, factor)


def split(x, parts):
    terms = []
    for _ in range(parts - 1):
        term = x.astype(BF16)
        terms.append(term)
        x = x - term.astype(F32)
    terms.append(x.astype(BF16))
    return terms


def exchange_kernel(
    sizes, dev, group, position, pressure, saturation, shape_factor, mine, other,
    drop_out, upwind_out, own_sums, other_sums, state, picks, terms,
):
    members, tiles, rows, width = sizes
    half = mine.shape[0]
    total = 2 * half
    group_tiles = members * tiles
    relative = group[...] ^ (dev[0] // members)
    index = (
        (relative & 1) * half
        + (relative >> 1) * group_tiles
        + (position[...] ^ ((dev[0] % members) * tiles))
    )
    step = min(256, half)
    for source, base in ((mine, 0), (other, half)):
        for start in range(0, half, step):
            for lane, lift in ((0, LIFT), (width, 1.0)):
                values = source[start : start + step, lane : lane + width] * lift
                for k, term in enumerate(split(values, 3)):
                    column = (3 if lane else 0) * width + k * width
                    state[base + start : base + start + step, column : column + width] = term
    lanes = lax.broadcasted_iota(jnp.int32, (128, 128), 1)
    block = 256
    for start in range(0, rows, block):
        for sub in range(0, block, 128):
            spread = jnp.broadcast_to(index[:, start + sub : start + sub + 128], (128, 128)).T
            for column in range(0, total, 128):
                picks[sub : sub + 128, column : column + 128] = jnp.where(
                    spread == lanes + column, 1.0, 0.0
                ).astype(BF16)
        found = jnp.dot(picks[...], state[...], preferred_element_type=F32)
        here = slice(start, start + block)
        other_pressure = (
            (found[:, :width] + found[:, width : 2 * width]) + found[:, 2 * width : 3 * width]
        ) * (1.0 / LIFT)
        other_saturation = (
            found[:, 3 * width : 4 * width] + found[:, 4 * width : 5 * width]
        ) + found[:, 5 * width :]
        drop = pressure[here, :] - other_pressure
        upwind = jnp.where(drop >= 0.0, saturation[here, :], other_saturation)
        water_mob, oil_mob = mobility(upwind)
        factor = shape_factor[here, :] * drop
        drop_out[here, :] = drop
        upwind_out[here, :] = upwind
        for k, flow in enumerate((factor * water_mob, factor * oil_mob)):
            high, low = split(flow, 2)
            terms[here, 2 * k * width : (2 * k + 1) * width] = high
            terms[here, (2 * k + 1) * width : (2 * k + 2) * width] = low
    sublanes = lax.broadcasted_iota(jnp.int32, (step, rows), 0)
    for target, base in ((other_sums, half), (own_sums, 0)):
        for start in range(0, half, step):
            owned = jnp.where(index == sublanes + (base + start), 1.0, 0.0).astype(BF16)
            sums = jnp.dot(owned, terms[...], preferred_element_type=F32)
            target[start : start + step, :width] = sums[:, :width] + sums[:, width : 2 * width]
            target[start : start + step, width:] = (
                sums[:, 2 * width : 3 * width] + sums[:, 3 * width :]
            )


def matrix_kernel(
    pressure, saturation, pressure_old, saturation_old, pore, shape_factor, drop_in, upwind_in,
    residual, jacobian, top,
):
    drop = drop_in[...]
    sat = saturation[...]
    vol = pore[...]
    csf = shape_factor[...]
    store_water, store_oil, factor = storage(
        pressure[...], sat, pressure_old[...], saturation_old[...], vol
    )
    water_mob, oil_mob = mobility(upwind_in[...])
    upstream = drop >= 0.0
    water = store_water + csf * water_mob * drop
    oil = store_oil + csf * oil_mob * drop
    residual[0] = water
    residual[1] = oil
    jacobian[0] = vol * ROCK_COMPRESS * sat + csf * water_mob
    jacobian[1] = vol * factor + jnp.where(upstream, csf * 2.0 * sat / VISC_WATER * drop, 0.0)
    jacobian[2] = vol * ROCK_COMPRESS * (1.0 - sat) + csf * oil_mob
    jacobian[3] = -vol * factor + jnp.where(
        upstream, -csf * 2.0 * (1.0 - sat) / VISC_OIL * drop, 0.0
    )

    @pl.when(pl.program_id(0) == 0)
    def _():
        top[...] = jnp.zeros_like(top)

    for k, values in enumerate((water, oil)):
        largest = jnp.max(jnp.abs(values), axis=0, keepdims=True)
        top[k : k + 1, :] = jnp.maximum(top[k : k + 1, :], largest)


def fracture_kernel(
    pressure, saturation, pressure_old, saturation_old, pore, trans, matrix_top, *rest
):
    pieces, (residual, tops) = rest[:-2], rest[-2:]
    width = pressure.shape[1]
    p, s = pressure[...], saturation[...]
    water, oil, _ = storage(p, s, pressure_old[...], saturation_old[...], pore[...])
    lane = lax.broadcasted_iota(jnp.int32, p.shape, 1)
    drop = p - pltpu.roll(p, width - 1, 1)
    upwind = jnp.where(drop >= 0.0, s, pltpu.roll(s, width - 1, 1))
    sums = pieces[0][...]
    for piece in pieces[1:]:
        sums = sums + piece[...]
    for k, (stored, mob) in enumerate(zip((water, oil), mobility(upwind))):
        link = jnp.where(lane < width - 1, trans[...] * mob * drop, 0.0)
        net = link - jnp.where(lane > 0, pltpu.roll(link, 1, 1), 0.0)
        values = stored + net - sums[:, k * width : (k + 1) * width]
        residual[k] = values
        largest = jnp.max(jnp.abs(values), axis=0, keepdims=True)
        largest = jnp.maximum(largest, matrix_top[k : k + 1, :])
        tops[:, k : k + 1, :] = jnp.broadcast_to(largest[None], (tops.shape[0], 1, width))


def scale_kernel(tops, matrix, fracture, matrix_out, fracture_out):
    for k in range(2):
        scale = 1.0 / (jnp.max(tops[:, k, :], keepdims=True) + EPSILON)
        matrix_out[k] = matrix[k] * scale
        fracture_out[k] = fracture[k] * scale


def per_device(
    matrix_pressure_iterate,
    matrix_water_saturation,
    matrix_pressure_prior,
    matrix_saturation_prior,
    matrix_pore_volume,
    cell_shape_factor,
    fracture_pressure,
    fracture_saturation,
    fracture_pressure_old,
    fracture_saturation_old,
    fracture_pore,
    fracture_trans,
    feeding_owner_group,
    owner_tile_position,
):
    groups = lax.axis_size("cluster")
    members = lax.axis_size("matrix")
    rows, width = matrix_pressure_iterate.shape
    tiles = fracture_pressure.shape[0]
    group_tiles = members * tiles
    chips = groups // 2
    half = chips * group_tiles
    dev = (lax.axis_index("cluster") * members + lax.axis_index("matrix")).reshape(1)

    def swap(x, axis, bits):
        return lax.ppermute(x, axis, [(i, i ^ bits) for i in range(lax.axis_size(axis))])

    own = jnp.concatenate([fracture_pressure, fracture_saturation], axis=1)
    layer = jnp.concatenate([own] + [swap(own, "matrix", z) for z in range(1, members)], axis=0)
    mine = jnp.concatenate([layer] + [swap(layer, "cluster", 2 * c) for c in range(1, chips)], axis=0)
    other = swap(mine, "cluster", 1)
    drop, upwind, own_sums, other_sums = pl.pallas_call(
        functools.partial(exchange_kernel, (members, tiles, rows, width)),
        in_specs=[SMEM] + [VMEM] * 7,
        out_specs=[VMEM] * 4,
        out_shape=[struct(rows, width)] * 2 + [struct(half, 2 * width)] * 2,
        scratch_shapes=[
            pltpu.VMEM((2 * half, 6 * width), BF16),
            pltpu.VMEM((256, 2 * half), BF16),
            pltpu.VMEM((rows, 4 * width), BF16),
        ],
        compiler_params=params(24 if half <= 1024 else 60),
        name="exchange",
    )(
        dev,
        feeding_owner_group.reshape(1, rows),
        owner_tile_position.reshape(1, rows),
        matrix_pressure_iterate,
        matrix_water_saturation,
        cell_shape_factor,
        mine,
        other,
    )
    block = pl.BlockSpec((256, width), lambda i: (i, 0))
    residual, jacobian, matrix_top = pl.pallas_call(
        matrix_kernel,
        grid=(rows // 256,),
        in_specs=[block] * 8,
        out_specs=[
            pl.BlockSpec((2, 256, width), lambda i: (0, i, 0)),
            pl.BlockSpec((4, 256, width), lambda i: (0, i, 0)),
            pl.BlockSpec((2, width), lambda i: (0, 0)),
        ],
        out_shape=[struct(2, rows, width), struct(4, rows, width), struct(2, width)],
        compiler_params=params(24),
        cost_estimate=pl.CostEstimate(
            flops=40 * rows * width, bytes_accessed=56 * rows * width, transcendentals=0
        ),
        name="matrix",
    )(
        matrix_pressure_iterate,
        matrix_water_saturation,
        matrix_pressure_prior,
        matrix_saturation_prior,
        matrix_pore_volume,
        cell_shape_factor,
        drop,
        upwind,
    )
    chip_sums = own_sums + swap(other_sums, "cluster", 1)
    part = [chip_sums[c * group_tiles : (c + 1) * group_tiles] for c in range(chips)]
    layer_sums = part[0]
    for c in range(1, chips):
        layer_sums = layer_sums + swap(part[c], "cluster", 2 * c)
    part = [layer_sums[z * tiles : (z + 1) * tiles] for z in range(members)]
    pieces = [part[0]] + [swap(part[z], "matrix", z) for z in range(1, members)]
    fracture, tops = pl.pallas_call(
        fracture_kernel,
        in_specs=[VMEM] * (7 + members),
        out_specs=[VMEM] * 2,
        out_shape=[struct(2, tiles, width), struct(groups * members, 2, width)],
        compiler_params=params(8),
        name="fracture",
    )(
        fracture_pressure,
        fracture_saturation,
        fracture_pressure_old,
        fracture_saturation_old,
        fracture_pore,
        fracture_trans,
        matrix_top,
        *pieces,
    )
    tops = lax.all_to_all(tops, ("cluster", "matrix"), split_axis=0, concat_axis=0, tiled=True)
    matrix_residual, fracture_residual = pl.pallas_call(
        scale_kernel,
        in_specs=[VMEM] * 3,
        out_specs=[VMEM] * 2,
        out_shape=[struct(2, rows, width), struct(2, tiles, width)],
        compiler_params=params(8),
        name="scale",
    )(tops, residual, fracture)
    return (matrix_residual, fracture_residual, jacobian)


def solution(mesh):
    rows = P(("cluster", "matrix"), None)
    stacked = P(None, ("cluster", "matrix"), None)
    return jax.shard_map(
        per_device,
        mesh=mesh,
        in_specs=(rows,) * 13 + (P(("cluster", "matrix")),),
        out_specs=(stacked,) * 3,
        check_vma=False,
    )
```

time: 187 us -> 62 us (0.33)
  blocking collectives: 67.5 us -> 10 us
  waiting for transfers between devices: 64.6 us -> 19.6 us
  other arithmetic: 19.3 us -> 0.11 us
  between operations: 15.5 us -> 0.91 us
  starting transfers between devices: 5.27 us -> 17.5 us
  Pallas kernels: 0 us -> 7.24 us
  matrix products: 6.16 us -> 0 us
    all_gather x1 -> x0, waiting for transfers between devices: 47.1 us -> none  [per_device(): lax.all_gather(own_state, ('cluster', 'matrix'), axis=0, tiled=True)]
    pmax x1 -> x0, blocking collectives: 38.3 us -> none  [per_device(): lax.pmax(jnp.maximum(matrix_top, fracture_top), ('cluster', 'matrix'))]
    ppermute x0 -> x14, waiting for transfers between devices: none -> 19.6 us  [swap(): lax.ppermute(x, axis, [(i, i ^ bits) for i in range(lax.axis_size(axis))])]
    all_to_all x1, blocking collectives: 29.2 us -> 10 us  [per_device(): lax.all_to_all(tops, ('cluster', 'matrix'), split_axis=0, concat_axis=0,...]
    reduce_scatter x1 -> x0, waiting for transfers between devices: 17.5 us -> none  [per_device(): lax.psum_scatter(jnp.einsum('sf,sc->fc', lookup, arrived, precision=HIGHE...]
    ppermute x0 -> x14, starting transfers between devices: none -> 17.5 us  [swap(): lax.ppermute(x, axis, [(i, i ^ bits) for i in range(lax.axis_size(axis))])]
    pallas_call x0 -> x4, Pallas kernels: none -> 7.24 us  [the longest x1 3.39 us: per_device(): pl.pallas_call(functools.partial(exchange_kernel, (members, tiles, rows,...]
    another operation x8 -> x0, other arithmetic: 6.61 us -> none  [the longest x2 2.46 us: per_device(): jacobian = jnp.stack([jac_wp, jac_ws, jac_op, jac_os])]
  transfers between devices with their start and end apart: 3 -> 14, of which waited for: 2 -> 9; matrix products, arithmetic and copies ran while one was open for 11% -> 0% of each run, Pallas kernels for 0% -> 4%
where the time goes in v1:
time: 62 us; the launch traced here: 61.5 us
  waiting for transfers between devices  19.6 us (32%)
  starting transfers between devices  17.5 us (28%)
  blocking collectives  10 us (16%)
  Pallas kernels  7.24 us (12%)
  local copies, waits for them, and re-layouts  6.1 us (10%)
  between operations  0.91 us (1%)
    ppermute x14, waiting for transfers between devices, swap(): lax.ppermute(x, axis, [(i, i ^ bits) for i in range(lax.axis_size(axis))])  19.6 us
    ppermute x14, starting transfers between devices, swap(): lax.ppermute(x, axis, [(i, i ^ bits) for i in range(lax.axis_size(axis))])  17.5 us
    all_to_all x1, blocking collectives, per_device(): lax.all_to_all(tops, ('cluster', 'matrix'), split_axis=0, concat_axis=0,...  10 us
    unnamed x40, local copies, waits for them, and re-layouts  5.33 us
    pallas_call x1, Pallas kernels, per_device(): pl.pallas_call(functools.partial(exchange_kernel, (members, tiles, rows,...  3.39 us
    pallas_call x1, Pallas kernels, per_device(): pl.pallas_call(matrix_kernel, grid=(rows // 256,), in_specs=[block] * 8,...  2.5 us
  transfers between devices with their start and end apart: 14, of which 9 were waited for; matrix products, arithmetic and copies ran while one was open for 0% of the time, Pallas kernels for 4%

profile of v1, /device:TPU:0, one launch (start us, length us, event | category | flops | bytes accessed | tf_op | source)
XLA Modules:
  0.0 61.5 jit_solution(10694321246493271461)
XLA Ops:
  0.6 0.7 %constant_dynamic-update-slice_fusion.1 = (f32[32,256]{1,0:T(8,128)S(1)}, f32[512,256]{1,0:T(8,128)S(1)}) fusion(f32[32,128]{1,0:T(8,128)} %pressure.5), kind=kLoop, calls=%fused_computation.5 | loop fusion | bytes 49152
  1.4 0.7 %constant_dynamic-update-slice_fusion = (f32[32,256]{1,0:T(8,128)S(1)}, f32[512,256]{1,0:T(8,128)S(1)}) fusion(f32[32,256]{1,0:T(8,128)S(1)} %get-tuple-element.34, f32[32,128]{1,0:T(8,128)} %saturation.5, f32[512,256]{1,0:T(8,128)S(1)} %get-tuple-element.35), kind=kLoop, calls=%fused_computation.4 | loop fusion | bytes 49152 | tf_op jit(solution)/shard_map/concatenate | solution.py:205
  2.1 5.1 %collective-permute-start.2 = (f32[32,256]{1,0:T(8,128)S(1)}, f32[32,256]{1,0:T(8,128)S(1)}, u32[]{:S(2)}, u32[]{:S(2)}) collective-permute-start(f32[32,256]{1,0:T(8,128)S(1)} %get-tuple-element.32), channel_id=1, source_target_pairs={{0,3},{1,2},{2,1},{3,0},{4,7},{5,6},{6,5},{7,4},{8,11},{9,10},{10,... | collective-permute-start | bytes 98312 | tf_op jit(solution)/shard_map/ppermute | solution.py:203
  7.2 0.0 collective-permute-start.1
  7.2 0.6 collective-permute-start
  7.7 1.3 %collective-permute-done.2 = f32[32,256]{1,0:T(8,128)S(1)} collective-permute-done((f32[32,256]{1,0:T(8,128)S(1)}, f32[32,256]{1,0:T(8,128)S(1)}, u32[]{:S(2)}, u32[]{:S(2)}) %collective-permute-start.2) | collective-permute-done | bytes 32800 | tf_op jit(solution)/shard_map/ppermute | solution.py:203
  9.0 2.9 %collective-permute-done.1 = f32[32,256]{1,0:T(8,128)S(1)} collective-permute-done((f32[32,256]{1,0:T(8,128)S(1)}, f32[32,256]{1,0:T(8,128)S(1)}, u32[]{:S(2)}, u32[]{:S(2)}) %collective-permute-start.1) | collective-permute-done | bytes 32800 | tf_op jit(solution)/shard_map/ppermute | solution.py:203
  12.0 0.0 collective-permute-done
  12.0 2.5 %collective-permute-start.5 = (f32[128,256]{1,0:T(8,128)S(1)}, f32[128,256]{1,0:T(8,128)S(1)}, u32[]{:S(2)}, u32[]{:S(2)}) collective-permute-start(f32[128,256]{1,0:T(8,128)S(1)} %pad_maximum_fusion), channel_id=1, source_target_pairs={{0,24},{4,28},{8,16},{12,20},{16,8},{20,12},{24,0},{28,4},{1,25},{... | collective-permute-start | bytes 393224 | tf_op jit(solution)/shard_map/ppermute | solution.py:203
  14.5 0.5 collective-permute-start.4
  15.0 0.5 collective-permute-start.3
  15.6 4.4 %collective-permute-done.3 = f32[128,256]{1,0:T(8,128)S(1)} collective-permute-done((f32[128,256]{1,0:T(8,128)S(1)}, f32[128,256]{1,0:T(8,128)S(1)}, u32[]{:S(2)}, u32[]{:S(2)}) %collective-permute-start.3) | collective-permute-done | bytes 131104 | tf_op jit(solution)/shard_map/ppermute | solution.py:203
  20.0 0.1 collective-permute-done.4
  20.1 0.0 collective-permute-done.5
  20.1 0.1 collective-permute-start.6
  20.2 1.9 %collective-permute-done.6.other = f32[512,256]{1,0:T(8,128)S(1)} collective-permute-done((f32[512,256]{1,0:T(8,128)S(1)}, f32[512,256]{1,0:T(8,128)S(1)}, u32[]{:S(2)}, u32[]{:S(2)}) %collective-permute-start.6) | collective-permute-done | bytes 524320 | tf_op jit(solution)/shard_map/ppermute | solution.py:203
  22.1 1.0 %copy-done = f32[1024,128]{1,0:T(8,128)S(1)} copy-done((f32[1024,128]{1,0:T(8,128)S(1)}, f32[1024,128]{1,0:T(8,128)}, u32[]{:S(2)}) %copy-start) | copy-done | bytes 524312
  23.2 1.0 %copy-done.2 = f32[1024,128]{1,0:T(8,128)S(1)} copy-done((f32[1024,128]{1,0:T(8,128)S(1)}, f32[1024,128]{1,0:T(8,128)}, u32[]{:S(2)}) %copy-start.2) | copy-done | bytes 524312
  24.2 1.0 %copy-done.4 = f32[1024,128]{1,0:T(8,128)S(1)} copy-done((f32[1024,128]{1,0:T(8,128)S(1)}, f32[1024,128]{1,0:T(8,128)}, u32[]{:S(2)}) %copy-start.4) | copy-done | bytes 524312
  25.2 0.7 %copy-done.15 = s32[1024,1]{0,1:T(1,128)S(1)} copy-done((s32[1024,1]{0,1:T(1,128)S(1)}, s32[1024,1]{0,1:T(1,128)}, u32[]{:S(2)}) %copy-start.15) | copy-done | bytes 4120
  25.9 0.7 %copy-done.16 = s32[1024]{0:T(1024)S(1)} copy-done((s32[1024]{0:T(1024)S(1)}, s32[1024]{0:T(1024)}, u32[]{:S(2)}) %copy-start.16) | copy-done | bytes 4120
  26.6 3.4 %exchange.1 = (f32[1024,128]{1,0:T(8,128)S(1)}, f32[1024,128]{1,0:T(8,128)S(1)}, f32[512,256]{1,0:T(8,128)S(1)}, f32[512,256]{1,0:T(8,128)S(1)}) custom-call(s32[1]{0:T(128)} %bitcast.dev, s32[1,1024]{1,0:T(1,128)S(1)} %bitcast.3, s32[1,1024]{1,0:T(1,128)S(1)} %bitcast.4, f32[1024,128]{1,0:T(8,128)S(1)} %copy-done, f32[1024,128]{1,0:T(8,128)S(1)} %copy-done.2, ...), custom_call_target="tpu_custom_call" | custom-call | tf_op jit(solution)/shard_map/exchange/pallas_call | solution.py:209
  30.0 0.0 copy-start.1
  30.0 0.0 copy-start.3
  30.0 0.0 copy-start.5
  30.0 0.0 copy-start.6
  30.1 0.0 copy-start.7
  30.1 0.0 copy-start.8
  30.1 0.2 collective-permute-start.7
  30.3 1.8 %collective-permute-done.7 = f32[512,256]{1,0:T(8,128)S(1)} collective-permute-done((f32[512,256]{1,0:T(8,128)S(1)}, f32[512,256]{1,0:T(8,128)S(1)}, u32[]{:S(2)}, u32[]{:S(2)}) %collective-permute-start.7) | collective-permute-done | bytes 524320 | tf_op jit(solution)/shard_map/ppermute | solution.py:203
  32.1 0.1 add.16
  32.2 1.2 %collective-permute-start.8 = (f32[128,256]{1,0:T(8,128)S(1)}, f32[128,256]{1,0:T(8,128)S(1)}, u32[]{:S(2)}, u32[]{:S(2)}) collective-permute-start(f32[128,256]{1,0:T(8,128)S(1)} %get-tuple-element.25), channel_id=1, source_target_pairs={{0,8},{4,12},{8,0},{12,4},{16,24},{20,28},{24,16},{28,20},{1,9},{5... | collective-permute-start | bytes 393224 | tf_op jit(solution)/shard_map/ppermute | solution.py:203
  33.4 1.8 %collective-permute-start.10 = (f32[128,256]{1,0:T(8,128)S(1)}, f32[128,256]{1,0:T(8,128)S(1)}, u32[]{:S(2)}, u32[]{:S(2)}) collective-permute-start(f32[128,256]{1,0:T(8,128)S(1)} %get-tuple-element.26), channel_id=1, source_target_pairs={{0,24},{4,28},{8,16},{12,20},{16,8},{20,12},{24,0},{28,4},{1,25},{... | collective-permute-start | bytes 393224 | tf_op jit(solution)/shard_map/ppermute | solution.py:203
  35.1 0.6 collective-permute-start.9
  35.7 2.9 %collective-permute-done.8 = f32[128,256]{1,0:T(8,128)S(1)} collective-permute-done((f32[128,256]{1,0:T(8,128)S(1)}, f32[128,256]{1,0:T(8,128)S(1)}, u32[]{:S(2)}, u32[]{:S(2)}) %collective-permute-start.8) | collective-permute-done | bytes 131104 | tf_op jit(solution)/shard_map/ppermute | solution.py:203
  38.6 2.9 %collective-permute-done.10 = f32[128,256]{1,0:T(8,128)S(1)} collective-permute-done((f32[128,256]{1,0:T(8,128)S(1)}, f32[128,256]{1,0:T(8,128)S(1)}, u32[]{:S(2)}, u32[]{:S(2)}) %collective-permute-start.10) | collective-permute-done | bytes 131104 | tf_op jit(solution)/shard_map/ppermute | solution.py:203
  41.5 1.4 %collective-permute-done.9 = f32[128,256]{1,0:T(8,128)S(1)} collective-permute-done((f32[128,256]{1,0:T(8,128)S(1)}, f32[128,256]{1,0:T(8,128)S(1)}, u32[]{:S(2)}, u32[]{:S(2)}) %collective-permute-start.9) | collective-permute-done | bytes 131104 | tf_op jit(solution)/shard_map/ppermute | solution.py:203
  43.0 1.5 %collective-permute-start.13 = (f32[32,256]{1,0:T(8,128)S(1)}, f32[32,256]{1,0:T(8,128)S(1)}, u32[]{:S(2)}, u32[]{:S(2)}) collective-permute-start(f32[32,256]{1,0:T(8,128)S(1)} %get-tuple-element.28), channel_id=1, source_target_pairs={{0,3},{1,2},{2,1},{3,0},{4,7},{5,6},{6,5},{7,4},{8,11},{9,10},{10,... | collective-permute-start | bytes 98312 | tf_op jit(solution)/shard_map/ppermute | solution.py:203
  44.5 0.6 %collective-permute-start.12 = (f32[32,256]{1,0:T(8,128)S(1)}, f32[32,256]{1,0:T(8,128)S(1)}, u32[]{:S(2)}, u32[]{:S(2)}) collective-permute-start(f32[32,256]{1,0:T(8,128)S(1)} %get-tuple-element.29), channel_id=1, source_target_pairs={{0,2},{1,3},{2,0},{3,1},{4,6},{5,7},{6,4},{7,5},{8,10},{9,11},{10,... | collective-permute-start | bytes 98312 | tf_op jit(solution)/shard_map/ppermute | solution.py:203
  45.1 2.3 %collective-permute-start.11 = (f32[32,256]{1,0:T(8,128)S(1)}, f32[32,256]{1,0:T(8,128)S(1)}, u32[]{:S(2)}, u32[]{:S(2)}) collective-permute-start(f32[32,256]{1,0:T(8,128)S(1)} %get-tuple-element.30), channel_id=1, source_target_pairs={{0,1},{1,0},{2,3},{3,2},{4,5},{5,4},{6,7},{7,6},{8,9},{9,8},{10,11... | collective-permute-start | bytes 98312 | tf_op jit(solution)/shard_map/ppermute | solution.py:203
  47.4 0.0 copy-done.1
  47.4 0.0 copy-done.3
  47.4 0.0 copy-done.5
  47.4 0.0 copy-done.6
  47.4 0.0 copy-done.7
  47.4 0.0 copy-done.8
  47.5 0.0 copy-start.9
  47.5 0.0 copy-start.10
  47.5 0.0 copy-start.11
  47.5 0.0 copy-start.12
  47.5 0.0 copy-start.13
  47.5 0.0 copy-start.14
  47.5 2.5 %matrix.1 = (f32[2,1024,128]{2,1,0:T(8,128)S(1)}, f32[4,1024,128]{2,1,0:T(8,128)}, f32[2,128]{1,0:T(2,128)S(1)}) custom-call(f32[1024,128]{1,0:T(8,128)S(1)} %copy-done.1, f32[1024,128]{1,0:T(8,128)S(1)} %copy-done.3, f32[1024,128]{1,0:T(8,128)S(1)} %copy-done.6, f32[1024,128]{1,0:T(8,128)S(1)} %copy-done.7, f32[1024,128]{1,0:T(8,128)S(1)} %copy-done.8, ...), custom_call_target="tpu_custom_call" | custom-call | flops 5242880 | bytes 7340032 | tf_op jit(solution)/shard_map/matrix/pallas_call | solution.py:232
  50.0 0.0 collective-permute-done.13.rest_3_
  50.0 0.0 collective-permute-done.12.rest_2_
  50.0 0.0 collective-permute-done.11.rest_1_
  50.0 0.0 copy-done.9
  50.0 0.0 copy-done.10
  50.1 0.0 copy-done.11
  50.1 0.0 copy-done.12
  50.1 0.0 copy-done.13
  50.1 0.2 fracture.1
  50.3 10.0 %all_to_all.5.tops = f32[32,2,128]{2,1,0:T(2,128)S(1)} all-to-all(f32[32,2,128]{2,1,0:T(2,128)S(1)} %get-tuple-element.19), channel_id=1, replica_groups=mesh['cluster'=8,'matrix'=4] {'cluster','matrix'}, dimensions={0} | all-to-all | bytes 65536 | tf_op jit(solution)/shard_map/all_to_all | solution.py:281
  60.3 1.2 %scale.1 = (f32[2,1024,128]{2,1,0:T(8,128)}, f32[2,32,128]{2,1,0:T(8,128)}) custom-call(f32[32,2,128]{2,1,0:T(2,128)S(1)} %all_to_all.5.tops, f32[2,1024,128]{2,1,0:T(8,128)S(1)} %get-tuple-element.20.matrix, f32[2,32,128]{2,1,0:T(8,128)S(1)} %get-tuple-element.21.fracture), custom_call_target="tpu_custom_call" | custom-call | tf_op jit(solution)/shard_map/scale/pallas_call | solution.py:282
  (16 shorter events, 0.1 us)
Async XLA Ops:
  2.1 7.0 %collective-permute-start.2 = (f32[32,256]{1,0:T(8,128)S(1)}, f32[32,256]{1,0:T(8,128)S(1)}, u32[]{:S(2)}, u32[]{:S(2)}) collective-permute-start(f32[32,256]{1,0:T(8,128)S(1)} %get-tuple-element.32), channel_id=1, source_target_pairs={{0,3},{1,2},{2,1},{3,0},{4,7},{5,6},{6,5},{7,4},{8,11},{9,10},{10,... | collective-permute-start | bytes 98312 | tf_op jit(solution)/shard_map/ppermute | solution.py:203
  7.2 4.8 %collective-permute-start.1 = (f32[32,256]{1,0:T(8,128)S(1)}, f32[32,256]{1,0:T(8,128)S(1)}, u32[]{:S(2)}, u32[]{:S(2)}) collective-permute-start(f32[32,256]{1,0:T(8,128)S(1)} %get-tuple-element.32), channel_id=1, source_target_pairs={{0,2},{1,3},{2,0},{3,1},{4,6},{5,7},{6,4},{7,5},{8,10},{9,11},{10,... | collective-permute-start | bytes 98312 | tf_op jit(solution)/shard_map/ppermute | solution.py:203
  7.2 4.8 %collective-permute-start = (f32[32,256]{1,0:T(8,128)S(1)}, f32[32,256]{1,0:T(8,128)S(1)}, u32[]{:S(2)}, u32[]{:S(2)}) collective-permute-start(f32[32,256]{1,0:T(8,128)S(1)} %get-tuple-element.32), channel_id=1, source_target_pairs={{0,1},{1,0},{2,3},{3,2},{4,5},{5,4},{6,7},{7,6},{8,9},{9,8},{10,11... | collective-permute-start | bytes 98312 | tf_op jit(solution)/shard_map/ppermute | solution.py:203
  12.0 8.1 %collective-permute-start.5 = (f32[128,256]{1,0:T(8,128)S(1)}, f32[128,256]{1,0:T(8,128)S(1)}, u32[]{:S(2)}, u32[]{:S(2)}) collective-permute-start(f32[128,256]{1,0:T(8,128)S(1)} %pad_maximum_fusion), channel_id=1, source_target_pairs={{0,24},{4,28},{8,16},{12,20},{16,8},{20,12},{24,0},{28,4},{1,25},{... | collective-permute-start | bytes 393224 | tf_op jit(solution)/shard_map/ppermute | solution.py:203
  14.5 5.6 %collective-permute-start.4 = (f32[128,256]{1,0:T(8,128)S(1)}, f32[128,256]{1,0:T(8,128)S(1)}, u32[]{:S(2)}, u32[]{:S(2)}) collective-permute-start(f32[128,256]{1,0:T(8,128)S(1)} %pad_maximum_fusion), channel_id=1, source_target_pairs={{0,16},{4,20},{8,24},{12,28},{16,0},{20,4},{24,8},{28,12},{1,17},{... | collective-permute-start | bytes 393224 | tf_op jit(solution)/shard_map/ppermute | solution.py:203
  15.0 5.0 %collective-permute-start.3 = (f32[128,256]{1,0:T(8,128)S(1)}, f32[128,256]{1,0:T(8,128)S(1)}, u32[]{:S(2)}, u32[]{:S(2)}) collective-permute-start(f32[128,256]{1,0:T(8,128)S(1)} %pad_maximum_fusion), channel_id=1, source_target_pairs={{0,8},{4,12},{8,0},{12,4},{16,24},{20,28},{24,16},{28,20},{1,9},{5... | collective-permute-start | bytes 393224 | tf_op jit(solution)/shard_map/ppermute | solution.py:203
  20.1 2.0 %collective-permute-start.6 = (f32[512,256]{1,0:T(8,128)S(1)}, f32[512,256]{1,0:T(8,128)S(1)}, u32[]{:S(2)}, u32[]{:S(2)}) collective-permute-start(f32[512,256]{1,0:T(8,128)S(1)} %constant_dynamic-update-slice_fusion.2.mine), channel_id=1, source_target_pairs={{0,4},{4,0},{8,12},{12,8},{16,20},{20,16},{24,28},{28,24},{1,5},{5... | collective-permute-start | bytes 1572872 | tf_op jit(solution)/shard_map/ppermute | solution.py:203
  22.1 1.0 %copy-start = (f32[1024,128]{1,0:T(8,128)S(1)}, f32[1024,128]{1,0:T(8,128)}, u32[]{:S(2)}) copy-start(f32[1024,128]{1,0:T(8,128)} %pressure.4) | copy-start | bytes 1572868
  23.2 1.0 %copy-start.2 = (f32[1024,128]{1,0:T(8,128)S(1)}, f32[1024,128]{1,0:T(8,128)}, u32[]{:S(2)}) copy-start(f32[1024,128]{1,0:T(8,128)} %saturation.4) | copy-start | bytes 1572868
  24.2 1.0 %copy-start.4 = (f32[1024,128]{1,0:T(8,128)S(1)}, f32[1024,128]{1,0:T(8,128)}, u32[]{:S(2)}) copy-start(f32[1024,128]{1,0:T(8,128)} %shape_factor.3) | copy-start | bytes 1572868
  25.2 0.7 %copy-start.15 = (s32[1024,1]{0,1:T(1,128)S(1)}, s32[1024,1]{0,1:T(1,128)}, u32[]{:S(2)}) copy-start(s32[1024,1]{0,1:T(1,128)} %param.26) | copy-start | bytes 12292
  25.9 0.7 %copy-start.16 = (s32[1024]{0:T(1024)S(1)}, s32[1024]{0:T(1024)}, u32[]{:S(2)}) copy-start(s32[1024]{0:T(1024)} %param.27) | copy-start | bytes 12292
  30.0 17.4 %copy-start.1 = (f32[1024,128]{1,0:T(8,128)S(1)}, f32[1024,128]{1,0:T(8,128)}, u32[]{:S(2)}) copy-start(f32[1024,128]{1,0:T(8,128)} %pressure.4) | copy-start | bytes 1572868
  30.0 17.4 %copy-start.3 = (f32[1024,128]{1,0:T(8,128)S(1)}, f32[1024,128]{1,0:T(8,128)}, u32[]{:S(2)}) copy-start(f32[1024,128]{1,0:T(8,128)} %saturation.4) | copy-start | bytes 1572868
  30.0 17.4 %copy-start.5 = (f32[1024,128]{1,0:T(8,128)S(1)}, f32[1024,128]{1,0:T(8,128)}, u32[]{:S(2)}) copy-start(f32[1024,128]{1,0:T(8,128)} %shape_factor.3) | copy-start | bytes 1572868
  30.0 17.4 %copy-start.6 = (f32[1024,128]{1,0:T(8,128)S(1)}, f32[1024,128]{1,0:T(8,128)}, u32[]{:S(2)}) copy-start(f32[1024,128]{1,0:T(8,128)} %pressure_old.2) | copy-start | bytes 1572868
  30.1 17.4 %copy-start.7 = (f32[1024,128]{1,0:T(8,128)S(1)}, f32[1024,128]{1,0:T(8,128)}, u32[]{:S(2)}) copy-start(f32[1024,128]{1,0:T(8,128)} %saturation_old.2) | copy-start | bytes 1572868
  30.1 17.4 %copy-start.8 = (f32[1024,128]{1,0:T(8,128)S(1)}, f32[1024,128]{1,0:T(8,128)}, u32[]{:S(2)}) copy-start(f32[1024,128]{1,0:T(8,128)} %pore.2) | copy-start | bytes 1572868
  30.1 2.0 %collective-permute-start.7 = (f32[512,256]{1,0:T(8,128)S(1)}, f32[512,256]{1,0:T(8,128)S(1)}, u32[]{:S(2)}, u32[]{:S(2)}) collective-permute-start(f32[512,256]{1,0:T(8,128)S(1)} %get-tuple-element.18), channel_id=1, source_target_pairs={{0,4},{4,0},{8,12},{12,8},{16,20},{20,16},{24,28},{28,24},{1,5},{5... | collective-permute-start | bytes 1572872 | tf_op jit(solution)/shard_map/ppermute | solution.py:203
  32.2 6.4 %collective-permute-start.8 = (f32[128,256]{1,0:T(8,128)S(1)}, f32[128,256]{1,0:T(8,128)S(1)}, u32[]{:S(2)}, u32[]{:S(2)}) collective-permute-start(f32[128,256]{1,0:T(8,128)S(1)} %get-tuple-element.25), channel_id=1, source_target_pairs={{0,8},{4,12},{8,0},{12,4},{16,24},{20,28},{24,16},{28,20},{1,9},{5... | collective-permute-start | bytes 393224 | tf_op jit(solution)/shard_map/ppermute | solution.py:203
  33.4 8.2 %collective-permute-start.10 = (f32[128,256]{1,0:T(8,128)S(1)}, f32[128,256]{1,0:T(8,128)S(1)}, u32[]{:S(2)}, u32[]{:S(2)}) collective-permute-start(f32[128,256]{1,0:T(8,128)S(1)} %get-tuple-element.26), channel_id=1, source_target_pairs={{0,24},{4,28},{8,16},{12,20},{16,8},{20,12},{24,0},{28,4},{1,25},{... | collective-permute-start | bytes 393224 | tf_op jit(solution)/shard_map/ppermute | solution.py:203
  35.1 7.8 %collective-permute-start.9 = (f32[128,256]{1,0:T(8,128)S(1)}, f32[128,256]{1,0:T(8,128)S(1)}, u32[]{:S(2)}, u32[]{:S(2)}) collective-permute-start(f32[128,256]{1,0:T(8,128)S(1)} %get-tuple-element.27), channel_id=1, source_target_pairs={{0,16},{4,20},{8,24},{12,28},{16,0},{20,4},{24,8},{28,12},{1,17},{... | collective-permute-start | bytes 393224 | tf_op jit(solution)/shard_map/ppermute | solution.py:203
  43.0 7.1 %collective-permute-start.13 = (f32[32,256]{1,0:T(8,128)S(1)}, f32[32,256]{1,0:T(8,128)S(1)}, u32[]{:S(2)}, u32[]{:S(2)}) collective-permute-start(f32[32,256]{1,0:T(8,128)S(1)} %get-tuple-element.28), channel_id=1, source_target_pairs={{0,3},{1,2},{2,1},{3,0},{4,7},{5,6},{6,5},{7,4},{8,11},{9,10},{10,... | collective-permute-start | bytes 98312 | tf_op jit(solution)/shard_map/ppermute | solution.py:203
  44.5 5.5 %collective-permute-start.12 = (f32[32,256]{1,0:T(8,128)S(1)}, f32[32,256]{1,0:T(8,128)S(1)}, u32[]{:S(2)}, u32[]{:S(2)}) collective-permute-start(f32[32,256]{1,0:T(8,128)S(1)} %get-tuple-element.29), channel_id=1, source_target_pairs={{0,2},{1,3},{2,0},{3,1},{4,6},{5,7},{6,4},{7,5},{8,10},{9,11},{10,... | collective-permute-start | bytes 98312 | tf_op jit(solution)/shard_map/ppermute | solution.py:203
  45.1 4.9 %collective-permute-start.11 = (f32[32,256]{1,0:T(8,128)S(1)}, f32[32,256]{1,0:T(8,128)S(1)}, u32[]{:S(2)}, u32[]{:S(2)}) collective-permute-start(f32[32,256]{1,0:T(8,128)S(1)} %get-tuple-element.30), channel_id=1, source_target_pairs={{0,1},{1,0},{2,3},{3,2},{4,5},{5,4},{6,7},{7,6},{8,9},{9,8},{10,11... | collective-permute-start | bytes 98312 | tf_op jit(solution)/shard_map/ppermute | solution.py:203
  47.5 2.6 %copy-start.9 = (f32[32,128]{1,0:T(8,128)S(1)}, f32[32,128]{1,0:T(8,128)}, u32[]{:S(2)}) copy-start(f32[32,128]{1,0:T(8,128)} %pressure.5) | copy-start | bytes 49156
  47.5 2.6 %copy-start.10 = (f32[32,128]{1,0:T(8,128)S(1)}, f32[32,128]{1,0:T(8,128)}, u32[]{:S(2)}) copy-start(f32[32,128]{1,0:T(8,128)} %saturation.5) | copy-start | bytes 49156
  47.5 2.6 %copy-start.11 = (f32[32,128]{1,0:T(8,128)S(1)}, f32[32,128]{1,0:T(8,128)}, u32[]{:S(2)}) copy-start(f32[32,128]{1,0:T(8,128)} %pressure_old.3) | copy-start | bytes 49156
  47.5 2.6 %copy-start.12 = (f32[32,128]{1,0:T(8,128)S(1)}, f32[32,128]{1,0:T(8,128)}, u32[]{:S(2)}) copy-start(f32[32,128]{1,0:T(8,128)} %saturation_old.3) | copy-start | bytes 49156
  47.5 2.6 %copy-start.13 = (f32[32,128]{1,0:T(8,128)S(1)}, f32[32,128]{1,0:T(8,128)}, u32[]{:S(2)}) copy-start(f32[32,128]{1,0:T(8,128)} %pore.3) | copy-start | bytes 49156
  47.5 2.6 %copy-start.14 = (f32[32,128]{1,0:T(8,128)S(1)}, f32[32,128]{1,0:T(8,128)}, u32[]{:S(2)}) copy-start(f32[32,128]{1,0:T(8,128)} %trans.1) | copy-start | bytes 49156
